TPU v7x, 32 devices: a whole 2x2x4 slice. The times are simulated.
32 devices in a mesh: heads: 16 (over z, y, core), width: 2 (over x).
Axes of the slice: x: 2, y: 2, z: 4, core: 2. Of those that a mesh axis runs over, the one named last changes fastest.
Arguments:
- out_grad: bfloat16 [512, 7168], P('heads', 'width'), may hold values from -24 to 24
- w_out: float32 [4096, 7168], P('heads', 'width'), may hold values from -0.09375 to 0.09375
- row_moment: float32 [4096], P('heads'), may hold values from 4 to 400
- col_moment: float32 [7168], P('width'), may hold values from 4 to 400
- queries: bfloat16 [512, 6144], P('width', 'heads'), may hold values from -240 to 240
- latent: bfloat16 [512, 512], P('width'), may hold values from -6 to 6
- key_rope: bfloat16 [512, 64], P('width'), may hold values from -4 to 4
- w_kv_up: bfloat16 [512, 8192], P(None, 'heads'), may hold values from -0.25 to 0.25
- doc_lengths: int32 [2, 4], P('width'), may hold values from 1 to 160, 256 in all within a row
Outputs:
- weight_update: float32 [4096, 7168], P('heads', 'width')
- query_grad: bfloat16 [512, 6144], P('width', 'heads')
- latent_grad: float32 [512, 576], P('width', 'heads')
- kv_up_grad: float32 [512, 8192], P('width', 'heads')
Inputs may be any that keep to these rules, and one draw needn't show every extreme that they name: `doc_lengths`: row p holds the lengths of the 4 documents packed in order into pack p; they sum to 256 and the longest in every row is exactly 160.
All inputs are finite; a program needn't handle non-finite values.
Results may differ from a plain program's by a relative error of at most 0.0088.
Values may be sent and summed in bfloat16 or wider, within the bound.
No kernel may reach another device: no remote copies, remote signals or barrier semaphores. Data moves between devices by JAX's collectives and lax.ppermute only.
A program may use at most 64 MiB of HBM per device.

v0:
```python
import jax
import jax.numpy as jnp
from jax import lax
from jax.sharding import PartitionSpec as P

D = 7168
VD = 128
NOPE = 128
ROPE = 64
moment_decay = 0.9
update_eps = 1e-06


def doc_mask(lengths, length):
    doc_ends = jnp.cumsum(lengths)
    position = jnp.arange(length, dtype=jnp.int32)
    document = jnp.sum((position[:, None] >= doc_ends[None, :]).astype(jnp.int32), axis=1)
    return (document[:, None] == document[None, :]) & (position[None, :] <= position[:, None])


def forward_pack(queries, latent, key_rope, w_kv_up, allowed):
    length = queries.shape[0]
    n_heads = w_kv_up.shape[1] // (NOPE + VD)
    scale_factor = (NOPE + ROPE) ** (-0.5)
    key_value = jnp.dot(latent, w_kv_up, preferred_element_type=jnp.float32).astype(jnp.bfloat16)
    key_value = key_value.reshape(length, n_heads, NOPE + VD)
    key_nope = key_value[:, :, :NOPE]
    values = key_value[:, :, NOPE:]
    query_heads = queries.reshape(length, n_heads, NOPE + ROPE)
    scores = jnp.einsum(
        "ihd,jhd->hij", query_heads[:, :, :NOPE], key_nope, preferred_element_type=jnp.float32
    )
    scores = scores + jnp.einsum(
        "ihd,jd->hij", query_heads[:, :, NOPE:], key_rope, preferred_element_type=jnp.float32
    )
    scores = scores * scale_factor
    masked = jnp.where(allowed[None], scores, -jnp.inf)
    highest = jnp.max(masked, axis=2, keepdims=True)
    weights = jnp.exp(masked - highest)
    prob_full = weights / jnp.sum(weights, axis=2, keepdims=True)
    probs_half = prob_full.astype(jnp.bfloat16)
    attended = jnp.einsum("hij,jhd->ihd", probs_half, values, preferred_element_type=jnp.float32)
    attended = attended.astype(jnp.bfloat16).reshape(length, n_heads * VD)
    return (query_heads, key_nope, values, prob_full, probs_half, attended)


def backward_pack(states, attn_half, key_rope, w_kv_up):
    query_heads, key_nope, values, prob_full, probs_half, attended = states
    length = query_heads.shape[0]
    n_heads = query_heads.shape[1]
    scale_factor = (NOPE + ROPE) ** (-0.5)
    grad_heads = attn_half.reshape(length, n_heads, VD)
    row_delta = jnp.sum(
        grad_heads.astype(jnp.float32) * attended.reshape(length, n_heads, VD).astype(jnp.float32),
        axis=2,
    ).T
    prob_grad = jnp.einsum("ihd,jhd->hij", grad_heads, values, preferred_element_type=jnp.float32)
    score_grad = (prob_full * (prob_grad - row_delta[:, :, None]) * scale_factor).astype(
        jnp.bfloat16
    )
    nope_grad = jnp.einsum("hij,jhd->ihd", score_grad, key_nope, preferred_element_type=jnp.float32)
    rotary_grad = jnp.einsum(
        "hij,jd->ihd", score_grad, key_rope, preferred_element_type=jnp.float32
    )
    query_grad = jnp.concatenate([nope_grad, rotary_grad], axis=2).astype(jnp.bfloat16)
    query_grad = query_grad.reshape(length, n_heads * (NOPE + ROPE))
    key_nope_grad = jnp.einsum(
        "hij,ihd->jhd", score_grad, query_heads[:, :, :NOPE], preferred_element_type=jnp.float32
    )
    rope_grad = jnp.einsum(
        "hij,ihd->jd", score_grad, query_heads[:, :, NOPE:], preferred_element_type=jnp.float32
    )
    value_grad = jnp.einsum(
        "hij,ihd->jhd", probs_half, grad_heads, preferred_element_type=jnp.float32
    )
    kv_grad = jnp.concatenate([key_nope_grad, value_grad], axis=2).astype(jnp.bfloat16)
    kv_grad = kv_grad.reshape(length, n_heads * (NOPE + VD))
    latent_part = lax.dot_general(
        kv_grad, w_kv_up, (((1,), (1,)), ((), ())), preferred_element_type=jnp.float32
    )
    latent_term = jnp.concatenate([latent_part, rope_grad], axis=1)
    return (query_grad, latent_term, kv_grad)


def on_device(
    out_grad, w_out, row_moment, col_moment, queries, latent, key_rope, w_kv_up, doc_lengths
):
    length = queries.shape[0]
    allowed = doc_mask(doc_lengths[0], length)
    states = forward_pack(queries, latent, key_rope, w_kv_up, allowed)
    attended = states[5]
    w_half = w_out.astype(jnp.bfloat16)
    grad_rows = lax.all_gather(out_grad, "heads", axis=0, tiled=True)
    picked = grad_rows
    attn_grad = lax.psum_scatter(
        lax.dot_general(
            picked, w_half, (((1,), (1,)), ((), ())), preferred_element_type=jnp.float32
        ),
        "width",
        scatter_dimension=0,
        tiled=True,
    )
    attn_half = attn_grad.astype(jnp.bfloat16)
    picked = grad_rows
    gradient = lax.dot_general(
        lax.all_gather(attended, "width", axis=0, tiled=True),
        picked,
        (((0,), (0,)), ((), ())),
        preferred_element_type=jnp.float32,
    )
    query_grad, latent_term, kv_grad = backward_pack(states, attn_half, key_rope, w_kv_up)
    latent_grad = lax.psum_scatter(latent_term, "heads", scatter_dimension=1, tiled=True)
    picked = latent
    kv_up_grad = lax.psum_scatter(
        lax.dot_general(
            picked, kv_grad, (((0,), (0,)), ((), ())), preferred_element_type=jnp.float32
        ),
        "width",
        scatter_dimension=0,
        tiled=True,
    )
    squares = gradient * gradient
    row_part = jnp.sum(squares, axis=1)
    col_part = jnp.sum(squares, axis=0)
    row_count = gradient.shape[0]
    col_count = gradient.shape[1]
    rows_total = row_count * lax.axis_size("heads")
    head_index = lax.axis_index("heads")
    width_index = lax.axis_index("width")
    row_full = lax.dynamic_update_slice(
        jnp.zeros((rows_total,), jnp.float32), row_part, (head_index * row_count,)
    )
    col_full = lax.dynamic_update_slice(
        jnp.zeros((D,), jnp.float32), col_part, (width_index * col_count,)
    )
    row_all, col_all = lax.psum((row_full, col_full), ("heads", "width"))
    row_sum = lax.dynamic_slice_in_dim(row_all, head_index * row_count, row_count, 0)
    col_sum = lax.dynamic_slice_in_dim(col_all, width_index * col_count, col_count, 0)
    row_new = moment_decay * row_moment + (1.0 - moment_decay) * row_sum / D
    col_new = moment_decay * col_moment + (1.0 - moment_decay) * col_sum / rows_total
    scaled = gradient / jnp.sqrt(row_new[:, None] * col_new[None, :])
    mean_square = lax.psum(jnp.sum(scaled * scaled), ("heads", "width")) / (rows_total * D)
    weight_update = scaled / jnp.sqrt(mean_square + update_eps)
    return (weight_update, query_grad, latent_grad, kv_up_grad)


def solution(mesh):
    in_specs = (
        P("heads", "width"),
        P("heads", "width"),
        P("heads"),
        P("width"),
        P("width", "heads"),
        P("width", None),
        P("width", None),
        P(None, "heads"),
        P("width", None),
    )
    out_specs = (P("heads", "width"), P("width", "heads"), P("width", "heads"), P("width", "heads"))
    return jax.shard_map(
        on_device, mesh=mesh, in_specs=in_specs, out_specs=out_specs, check_vma=False
    )
```

profile of v0, /device:TPU:0, one launch (start us, length us, event | category | flops | bytes accessed | tf_op | source)
XLA Modules:
  0.0 205.8 jit_solution(9484889876110462075)
XLA Ops:
  7.2 0.7 all-gather.2.cloned.1.call-update
  8.0 1.1 copy.75
  9.0 1.2 convolution_convert_fusion
  10.7 0.8 reduce-window.8
  11.5 1.2 dynamic-slice
  12.8 47.9 %all-gather.2.cloned.1.call-done = bf16[512,3584]{1,0:T(8,128)(2,1)} async-done(((bf16[32,3584]{1,0:T(8,128)(2,1)}), bf16[512,3584]{1,0:T(8,128)(2,1)}) %all-gather.2.cloned.1.call-update) | async-done | bytes 3670032 | tf_op jit(solution)/shard_map/all_gather | solution.py:93
  60.7 5.1 %fusion.2 = f32[512,256]{1,0:T(8,128)} fusion(bf16[512,3584]{1,0:T(8,128)(2,1)} %all-gather.2.cloned.1.call-done, f32[256,3584]{1,0:T(8,128)} %param.10), kind=kOutput, calls=%fused_computation.6 | convolution fusion | flops 940441600 | bytes 7864320 | tf_op jit(solution)/shard_map/dot_general | solution.py:96
  66.3 0.3 fusion.10
  66.5 0.4 fusion.29
  66.9 12.4 %reduce-scatter.4.cloned.1.call-done = f32[256,256]{1,0:T(8,128)} async-done(((f32[512,256]{1,0:T(8,128)}), f32[256,256]{1,0:T(8,128)}) %reduce-scatter.4.cloned.1.call-update) | async-done | bytes 262160 | tf_op jit(solution)/shard_map/reduce_scatter | solution.py:95
  79.3 1.0 convert_element_type.46
  80.4 0.3 multiply_reduce_fusion.3
  80.7 0.3 fusion.14
  81.0 0.3 fusion.11
  81.2 0.2 fusion.13
  81.7 0.3 fusion.30
  82.1 0.9 pad_maximum_fusion
  83.0 5.7 %all_gather.6 = bf16[512,256]{0,1:T(8,128)(2,1)S(1)} all-gather(bf16[256,256]{0,1:T(8,128)(2,1)S(1)} %bitcast.69), channel_id=1, replica_groups=mesh['heads'=16,'width'=2] {'width'}, dimensions={0}, use_global_device_ids=true | all-gather | bytes 393216 | tf_op jit(solution)/shard_map/all_gather | solution.py:106
  88.8 5.1 %multiply_reduce_fusion.2 = (f32[256]{0:T(256)S(1)}, f32[3584]{0:T(1024)S(1)}, f32[256,3584]{1,0:T(8,128)}) fusion(bf16[512,256]{0,1:T(8,128)(2,1)S(1)} %all_gather.6, bf16[512,3584]{1,0:T(8,128)(2,1)} %all-gather.2.cloned.1.call-done), kind=kOutput, calls=%fused_computation.4 | convolution fusion | flops 942272768 | bytes 7617536 | tf_op jit(solution)/shard_map/dot_general | solution.py:105
  93.8 0.3 dynamic_update_slice.7
  94.2 0.3 dynamic_update_slice.6
  94.5 40.0 %all-reduce.1 = (f32[7168]{0:T(1024)S(1)}, f32[4096]{0:T(1024)S(1)}) all-reduce(f32[7168]{0:T(1024)S(1)} %dynamic_update_slice.7, f32[4096]{0:T(1024)S(1)} %dynamic_update_slice.6), channel_id=1, replica_groups=mesh['heads'=16,'width'=2] {'heads','width'}, use_global_device_ids=true, to_apply=%region_7.8 | all-reduce | flops 11264 | bytes 90112 | tf_op jit(solution)/shard_map/psum | solution.py:136
  134.6 1.3 convolution_bitcast_fusion
  136.0 3.7 %multiply_reduce_fusion = f32[]{:T(128)} fusion(f32[256,3584]{1,0:T(8,128)} %get-tuple-element.28, f32[3584]{0:T(1024)S(1)} %multiply_add_fusion, f32[256]{0:T(256)S(1)} %multiply_add_fusion.1), kind=kLoop, calls=%fused_computation.1 | loop fusion | flops 3670015 | bytes 3685380 | tf_op jit(solution)/shard_map/reduce_sum | solution.py:142
  140.3 41.3 %psum.23 = f32[]{:T(128)} all-reduce(f32[]{:T(128)} %multiply_reduce_fusion), channel_id=1, replica_groups=mesh['heads'=16,'width'=2] {'heads','width'}, use_global_device_ids=true, to_apply=%region_9.10 | all-reduce | flops 1 | bytes 8 | tf_op jit(solution)/shard_map/psum | solution.py:142
  181.7 0.2 fusion.12
  182.0 0.8 copy.90
  183.5 4.4 %fusion.1 = f32[256,3584]{1,0:T(8,128)} fusion(f32[256,3584]{1,0:T(8,128)} %get-tuple-element.28, f32[]{:T(128)S(6)} %sqrt.7, f32[3584]{0:T(1024)S(1)} %multiply_add_fusion, f32[256]{0:T(256)S(1)} %multiply_add_fusion.1), kind=kLoop, calls=%fused_computation.5 | loop fusion | flops 2752512 | bytes 7355396 | tf_op jit(solution)/shard_map/div | solution.py:143
  187.9 1.0 constant_dynamic-slice_fusion
  189.0 0.7 copy.91
  189.7 7.6 %reduce-scatter.6.cloned.1.call-done = f32[256,512]{0,1:T(8,128)} async-done(((f32[512,512]{0,1:T(8,128)}), f32[256,512]{0,1:T(8,128)}) %reduce-scatter.6.cloned.1.call-update) | async-done | bytes 524304 | tf_op jit(solution)/shard_map/reduce_scatter | solution.py:114
  197.2 2.0 copy.92
  (33 shorter events, 1.7 us)
Async XLA Ops:
  7.2 1.9 copy-start
  7.2 53.5 %all-gather.2.cloned.1.call-start = ((), (), s32[]{:S(2)}) async-start(), calls=%async_computation.2 | async-start | bytes 3899392 | tf_op jit(solution)/shard_map/all_gather | solution.py:93
  7.9 71.4 %reduce-scatter.4.cloned.1.call-start = ((), (), s32[]{:S(2)}) async-start(), calls=%async_computation.3 | async-start | bytes 786432 | tf_op jit(solution)/shard_map/reduce_scatter | solution.py:95
  12.8 53.5 %copy-start.2 = (bf16[256,64]{0,1:T(8,128)(2,1)S(1)}, bf16[256,64]{0,1:T(8,128)(2,1)}, u32[]{:S(2)}) copy-start(bf16[256,64]{0,1:T(8,128)(2,1)} %param.15) | copy-start | bytes 98308
  65.8 122.1 %all-reduce.4.cloned.1.call-start = ((), (), s32[]{:S(2)}) async-start(), calls=%async_computation.5 | async-start | bytes 1310720
  83.0 114.3 %reduce-scatter.6.cloned.1.call-start = ((), (), s32[]{:S(2)}) async-start(), calls=%async_computation.4 | async-start | bytes 1572864 | tf_op jit(solution)/shard_map/reduce_scatter | solution.py:114
  88.8 45.7 %copy-start.3 = (f32[3584]{0:T(1024)S(1)}, f32[3584]{0:T(1024)}, u32[]{:S(2)}) copy-start(f32[3584]{0:T(1024)} %param.12) | copy-start | bytes 43012
  88.8 45.8 %copy-start.4 = (f32[256]{0:T(256)S(1)}, f32[256]{0:T(256)}, u32[]{:S(2)}) copy-start(f32[256]{0:T(256)} %param.11) | copy-start | bytes 3076
  88.8 45.9 %copy-start.1 = (bf16[256,512]{1,0:T(8,128)(2,1)S(1)}, bf16[256,512]{1,0:T(8,128)(2,1)}, u32[]{:S(2)}) copy-start(bf16[256,512]{1,0:T(8,128)(2,1)} %param.14) | copy-start | bytes 786436
Sparse Core Ops, SparseCore 0:
  10.3 50.3 all-gather.1
  65.9 13.3 reduce-scatter.3
  83.1 91.8 all-reduce.3
  177.1 20.1 reduce-scatter.5
where the time goes:
time: 206 us
  blocking collectives  87 us (42%)
  waiting for transfers between devices  68.6 us (33%)
  between operations  15.3 us (7%)
  matrix products  15.2 us (7%)
  other arithmetic  11.6 us (6%)
  local copies, waits for them, and re-layouts  8.01 us (4%)
    all_gather x1, waiting for transfers between devices, on_device(): grad_rows = lax.all_gather(out_grad, 'heads', axis=0, tiled=True)  47.9 us
    psum x1, blocking collectives, on_device(): lax.psum(jnp.sum(scaled * scaled), ('heads', 'width')) / (rows_total * D)  41.3 us
    psum x1, blocking collectives, on_device(): row_all, col_all = lax.psum((row_full, col_full), ('heads', 'width'))  40 us
    reduce_scatter x1, waiting for transfers between devices, on_device(): lax.psum_scatter(lax.dot_general(picked, w_half, (((1,), (1,)), ((), ()))...  12.4 us
    reduce_scatter x1, waiting for transfers between devices, on_device(): lax.psum_scatter(lax.dot_general(picked, kv_grad, (((0,), (0,)), ((), ())...  7.56 us
    unnamed x17, local copies, waits for them, and re-layouts  7.03 us
    all_gather x1, blocking collectives, on_device(): lax.all_gather(attended, 'width', axis=0, tiled=True)  5.74 us
    dot_general x1, matrix products, on_device(): lax.dot_general(picked, w_half, (((1,), (1,)), ((), ())), preferred_eleme...  5.1 us
  transfers between devices with their start and end apart: 4, of which 3 were waited for; matrix products, arithmetic and copies ran while one was open for 12% of the time, Pallas kernels for 0%

commit v1 on v0

--- a/solution.py
+++ b/solution.py
@@ -90,7 +90,16 @@
     states = forward_pack(queries, latent, key_rope, w_kv_up, allowed)
     attended = states[5]
     w_half = w_out.astype(jnp.bfloat16)
-    grad_rows = lax.all_gather(out_grad, "heads", axis=0, tiled=True)
+    ways = lax.axis_size("heads")
+    up = [(d, (d + 1) % ways) for d in range(ways)]
+    down = [(d, (d - 1) % ways) for d in range(ways)]
+    earlier, later = ([out_grad], [out_grad])
+    for _ in range(ways // 2):
+        earlier.append(lax.ppermute(earlier[-1], "heads", up))
+    for _ in range((ways - 1) // 2):
+        later.append(lax.ppermute(later[-1], "heads", down))
+    line = jnp.concatenate([*earlier[::-1], *later[1:]], axis=0)
+    grad_rows = jnp.roll(line, (lax.axis_index("heads") - ways // 2) * out_grad.shape[0], axis=0)
     picked = grad_rows
     attn_grad = lax.psum_scatter(
         lax.dot_general(

time: 206 us -> 233 us (1.13)
  starting transfers between devices: 0.16 us -> 32.4 us
  waiting for transfers between devices: 68.6 us -> 49.6 us
  local copies, waits for them, and re-layouts: 8.01 us -> 23.7 us
  matrix products: 15.2 us -> 12 us
    all_gather x1 -> x0, waiting for transfers between devices: 47.9 us -> none  [on_device(): grad_rows = lax.all_gather(out_grad, 'heads', axis=0, tiled=True)]
    ppermute x0 -> x15, starting transfers between devices: none -> 32.3 us  [the longest x7 31.7 us: on_device(): later.append(lax.ppermute(later[-1], 'heads', down))]
    ppermute x0 -> x15, waiting for transfers between devices: none -> 29.6 us  [the longest x8 29.4 us: on_device(): earlier.append(lax.ppermute(earlier[-1], 'heads', up))]
    unnamed x17 -> x60, local copies, waits for them, and re-layouts: 7.03 us -> 22.6 us
    dot_general x1, matrix products: 5.1 us -> 1.94 us  [on_device(): lax.dot_general(picked, w_half, (((1,), (1,)), ((), ())), preferred_eleme...]
  transfers between devices with their start and end apart: 4 -> 18, of which waited for: 3 -> 11; matrix products, arithmetic and copies ran while one was open for 12% -> 13% of each run, Pallas kernels for 0% -> 0%
where the time goes in v1:
time: 233 us; the launch traced here: 232 us
  blocking collectives  87.3 us (37%)
  waiting for transfers between devices  49.6 us (21%)
  starting transfers between devices  32.4 us (14%)
  local copies, waits for them, and re-layouts  23.7 us (10%)
  between operations  15.7 us (7%)
  matrix products  12 us (5%)
  other arithmetic  11.8 us (5%)
    psum x1, blocking collectives, on_device(): lax.psum(jnp.sum(scaled * scaled), ('heads', 'width')) / (rows_total * D)  41.6 us
    psum x1, blocking collectives, on_device(): row_all, col_all = lax.psum((row_full, col_full), ('heads', 'width'))  40 us
    ppermute x7, starting transfers between devices, on_device(): later.append(lax.ppermute(later[-1], 'heads', down))  31.7 us
    ppermute x8, waiting for transfers between devices, on_device(): earlier.append(lax.ppermute(earlier[-1], 'heads', up))  29.4 us
    unnamed x60, local copies, waits for them, and re-layouts  22.6 us
    reduce_scatter x1, waiting for transfers between devices, on_device(): lax.psum_scatter(lax.dot_general(picked, w_half, (((1,), (1,)), ((), ()))...  11.4 us
    reduce_scatter x1, waiting for transfers between devices, on_device(): lax.psum_scatter(lax.dot_general(picked, kv_grad, (((0,), (0,)), ((), ())...  8.52 us
    all_gather x1, blocking collectives, on_device(): lax.all_gather(attended, 'width', axis=0, tiled=True)  5.76 us
  transfers between devices with their start and end apart: 18, of which 11 were waited for; matrix products, arithmetic and copies ran while one was open for 13% of the time, Pallas kernels for 0%

profile of v1, /device:TPU:0, one launch (start us, length us, event | category | flops | bytes accessed | tf_op | source)
XLA Modules:
  0.0 232.3 jit_solution(9840674544002927317)
XLA Ops:
  7.8 8.9 %collective-permute-done = bf16[32,3584]{1,0:T(8,128)(2,1)S(1)} collective-permute-done((bf16[32,3584]{1,0:T(8,128)(2,1)}, bf16[32,3584]{1,0:T(8,128)(2,1)S(1)}, u32[]{:S(2)}, u32[]{:S(2)}) %collective-permute-start) | collective-permute-done | bytes 229408 | tf_op jit(solution)/shard_map/ppermute | solution.py:98
  16.7 4.4 %collective-permute-start.8 = (bf16[32,3584]{1,0:T(8,128)(2,1)}, bf16[32,3584]{1,0:T(8,128)(2,1)S(1)}, u32[]{:S(2)}, u32[]{:S(2)}) collective-permute-start(bf16[32,3584]{1,0:T(8,128)(2,1)} %param.9), channel_id=1, source_target_pairs={{0,30},{2,0},{4,2},{6,4},{8,6},{10,8},{12,10},{14,12},{16,14},{18,... | collective-permute-start | bytes 688136 | tf_op jit(solution)/shard_map/ppermute | solution.py:100
  21.1 3.7 %collective-permute-done.1 = bf16[32,3584]{1,0:T(8,128)(2,1)S(1)} collective-permute-done((bf16[32,3584]{1,0:T(8,128)(2,1)S(1)}, bf16[32,3584]{1,0:T(8,128)(2,1)S(1)}, u32[]{:S(2)}, u32[]{:S(2)}) %collective-permute-start.1) | collective-permute-done | bytes 229408 | tf_op jit(solution)/shard_map/ppermute | solution.py:98
  25.0 4.6 %collective-permute-start.9 = (bf16[32,3584]{1,0:T(8,128)(2,1)S(1)}, bf16[32,3584]{1,0:T(8,128)(2,1)S(1)}, u32[]{:S(2)}, u32[]{:S(2)}) collective-permute-start(bf16[32,3584]{1,0:T(8,128)(2,1)S(1)} %collective-permute-done.8), channel_id=1, source_target_pairs={{0,30},{2,0},{4,2},{6,4},{8,6},{10,8},{12,10},{14,12},{16,14},{18,... | collective-permute-start | bytes 688136 | tf_op jit(solution)/shard_map/ppermute | solution.py:100
  29.6 3.5 %collective-permute-done.2 = bf16[32,3584]{1,0:T(8,128)(2,1)S(1)} collective-permute-done((bf16[32,3584]{1,0:T(8,128)(2,1)S(1)}, bf16[32,3584]{1,0:T(8,128)(2,1)S(1)}, u32[]{:S(2)}, u32[]{:S(2)}) %collective-permute-start.2) | collective-permute-done | bytes 229408 | tf_op jit(solution)/shard_map/ppermute | solution.py:98
  33.1 4.7 %collective-permute-start.10 = (bf16[32,3584]{1,0:T(8,128)(2,1)S(1)}, bf16[32,3584]{1,0:T(8,128)(2,1)S(1)}, u32[]{:S(2)}, u32[]{:S(2)}) collective-permute-start(bf16[32,3584]{1,0:T(8,128)(2,1)S(1)} %collective-permute-done.9), channel_id=1, source_target_pairs={{0,30},{2,0},{4,2},{6,4},{8,6},{10,8},{12,10},{14,12},{16,14},{18,... | collective-permute-start | bytes 688136 | tf_op jit(solution)/shard_map/ppermute | solution.py:100
  37.8 3.5 %collective-permute-done.3 = bf16[32,3584]{1,0:T(8,128)(2,1)S(1)} collective-permute-done((bf16[32,3584]{1,0:T(8,128)(2,1)S(1)}, bf16[32,3584]{1,0:T(8,128)(2,1)S(1)}, u32[]{:S(2)}, u32[]{:S(2)}) %collective-permute-start.3) | collective-permute-done | bytes 229408 | tf_op jit(solution)/shard_map/ppermute | solution.py:98
  41.4 4.7 %collective-permute-start.11 = (bf16[32,3584]{1,0:T(8,128)(2,1)S(1)}, bf16[32,3584]{1,0:T(8,128)(2,1)S(1)}, u32[]{:S(2)}, u32[]{:S(2)}) collective-permute-start(bf16[32,3584]{1,0:T(8,128)(2,1)S(1)} %collective-permute-done.10), channel_id=1, source_target_pairs={{0,30},{2,0},{4,2},{6,4},{8,6},{10,8},{12,10},{14,12},{16,14},{18,... | collective-permute-start | bytes 688136 | tf_op jit(solution)/shard_map/ppermute | solution.py:100
  46.1 3.5 %collective-permute-done.4 = bf16[32,3584]{1,0:T(8,128)(2,1)S(1)} collective-permute-done((bf16[32,3584]{1,0:T(8,128)(2,1)S(1)}, bf16[32,3584]{1,0:T(8,128)(2,1)S(1)}, u32[]{:S(2)}, u32[]{:S(2)}) %collective-permute-start.4) | collective-permute-done | bytes 229408 | tf_op jit(solution)/shard_map/ppermute | solution.py:98
  49.6 1.1 copy.75
  50.7 4.4 %collective-permute-start.12 = (bf16[32,3584]{1,0:T(8,128)(2,1)S(1)}, bf16[32,3584]{1,0:T(8,128)(2,1)}, u32[]{:S(2)}, u32[]{:S(2)}) collective-permute-start(bf16[32,3584]{1,0:T(8,128)(2,1)S(1)} %collective-permute-done.11), channel_id=1, source_target_pairs={{0,30},{2,0},{4,2},{6,4},{8,6},{10,8},{12,10},{14,12},{16,14},{18,... | collective-permute-start | bytes 688136 | tf_op jit(solution)/shard_map/ppermute | solution.py:100
  55.1 2.8 %collective-permute-done.5 = bf16[32,3584]{1,0:T(8,128)(2,1)} collective-permute-done((bf16[32,3584]{1,0:T(8,128)(2,1)S(1)}, bf16[32,3584]{1,0:T(8,128)(2,1)}, u32[]{:S(2)}, u32[]{:S(2)}) %collective-permute-start.5) | collective-permute-done | bytes 229408 | tf_op jit(solution)/shard_map/ppermute | solution.py:98
  57.9 1.2 convolution_convert_fusion
  60.1 4.4 %collective-permute-start.13 = (bf16[32,3584]{1,0:T(8,128)(2,1)}, bf16[32,3584]{1,0:T(8,128)(2,1)}, u32[]{:S(2)}, u32[]{:S(2)}) collective-permute-start(bf16[32,3584]{1,0:T(8,128)(2,1)} %collective-permute-done.12), channel_id=1, source_target_pairs={{0,30},{2,0},{4,2},{6,4},{8,6},{10,8},{12,10},{14,12},{16,14},{18,... | collective-permute-start | bytes 688136 | tf_op jit(solution)/shard_map/ppermute | solution.py:100
  64.6 1.8 collective-permute-done.6
  67.3 1.3 dynamic-slice
  68.6 4.4 %collective-permute-start.14 = (bf16[32,3584]{1,0:T(8,128)(2,1)}, bf16[32,3584]{1,0:T(8,128)(2,1)S(1)}, u32[]{:S(2)}, u32[]{:S(2)}) collective-permute-start(bf16[32,3584]{1,0:T(8,128)(2,1)} %collective-permute-done.13), channel_id=1, source_target_pairs={{0,30},{2,0},{4,2},{6,4},{8,6},{10,8},{12,10},{14,12},{16,14},{18,... | collective-permute-start | bytes 688136 | tf_op jit(solution)/shard_map/ppermute | solution.py:100
  73.1 1.7 collective-permute-done.7
  86.9 3.0 %copy-done.1 = bf16[1024,3584]{1,0:T(8,128)(2,1)} copy-done((bf16[1024,3584]{1,0:T(8,128)(2,1)}, bf16[1024,3584]{1,0:T(8,128)(2,1)S(1)}, u32[]{:S(2)}) %copy-start.1) | copy-done | bytes 7340056
  89.8 1.9 fusion.1
  92.9 11.4 %reduce-scatter.4.cloned.1.call-done = f32[256,256]{1,0:T(8,128)} async-done(((f32[512,256]{1,0:T(8,128)}), f32[256,256]{1,0:T(8,128)}) %reduce-scatter.4.cloned.1.call-update) | async-done | bytes 262160 | tf_op jit(solution)/shard_map/reduce_scatter | solution.py:104
  104.3 1.0 convert_element_type.46
  106.6 1.3 convolution_bitcast_fusion
  109.4 5.8 %all_gather.3 = bf16[512,256]{0,1:T(8,128)(2,1)S(1)} all-gather(bf16[256,256]{0,1:T(8,128)(2,1)S(1)} %bitcast.67), channel_id=1, replica_groups=mesh['heads'=16,'width'=2] {'width'}, dimensions={0}, use_global_device_ids=true | all-gather | bytes 393216 | tf_op jit(solution)/shard_map/all_gather | solution.py:115
  115.2 5.0 %multiply_reduce_fusion.2 = (f32[256]{0:T(256)S(1)}, f32[3584]{0:T(1024)S(1)}, f32[256,3584]{1,0:T(8,128)}) fusion(bf16[512,256]{0,1:T(8,128)(2,1)S(1)} %all_gather.3, bf16[1024,3584]{1,0:T(8,128)(2,1)} %copy-done.1, s32[]{:T(128)S(6)} %select_n.27), kind=kOutput, calls=%fused_computation.4 | convolution fusion | flops 942272768 | bytes 7617540 | tf_op jit(solution)/shard_map/dot_general | solution.py:114
  120.9 40.0 %all-reduce.1 = (f32[7168]{0:T(1024)S(1)}, f32[4096]{0:T(1024)S(1)}) all-reduce(f32[7168]{0:T(1024)S(1)} %dynamic_update_slice.7, f32[4096]{0:T(1024)S(1)} %dynamic_update_slice.6), channel_id=1, replica_groups=mesh['heads'=16,'width'=2] {'heads','width'}, use_global_device_ids=true, to_apply=%region_7.8 | all-reduce | flops 11264 | bytes 90112 | tf_op jit(solution)/shard_map/psum | solution.py:145
  161.0 3.7 %multiply_reduce_fusion = f32[]{:T(128)} fusion(f32[256,3584]{1,0:T(8,128)} %get-tuple-element.28, f32[3584]{0:T(1024)S(1)} %multiply_add_fusion, f32[256]{0:T(256)S(1)} %multiply_add_fusion.1), kind=kLoop, calls=%fused_computation.1 | loop fusion | flops 3670015 | bytes 3685380 | tf_op jit(solution)/shard_map/reduce_sum | solution.py:151
  165.4 41.6 %psum.23 = f32[]{:T(128)} all-reduce(f32[]{:T(128)} %multiply_reduce_fusion), channel_id=1, replica_groups=mesh['heads'=16,'width'=2] {'heads','width'}, use_global_device_ids=true, to_apply=%region_9.10 | all-reduce | flops 1 | bytes 8 | tf_op jit(solution)/shard_map/psum | solution.py:151
  208.9 4.6 %fusion.5 = f32[256,3584]{1,0:T(8,128)} fusion(f32[256,3584]{1,0:T(8,128)} %get-tuple-element.28, f32[]{:T(128)S(6)} %sqrt.7, f32[3584]{0:T(1024)S(1)} %multiply_add_fusion, f32[256]{0:T(256)S(1)} %multiply_add_fusion.1), kind=kLoop, calls=%fused_computation.9 | loop fusion | flops 2752512 | bytes 7355396 | tf_op jit(solution)/shard_map/div | solution.py:152
  213.5 1.0 constant_dynamic-slice_fusion
  215.3 8.5 %reduce-scatter.6.cloned.1.call-done = f32[256,512]{0,1:T(8,128)} async-done(((f32[512,512]{0,1:T(8,128)}), f32[256,512]{0,1:T(8,128)}) %reduce-scatter.6.cloned.1.call-update) | async-done | bytes 524304 | tf_op jit(solution)/shard_map/reduce_scatter | solution.py:123
  223.8 2.0 copy.92
  (104 shorter events, 21.2 us)
Async XLA Ops:
  7.2 50.7 %copy-start = (bf16[512,512]{1,0:T(8,128)(2,1)S(1)}, bf16[512,512]{1,0:T(8,128)(2,1)}, u32[]{:S(2)}) copy-start(bf16[512,512]{1,0:T(8,128)(2,1)} %param.16) | copy-start | bytes 1572868
  7.2 77.6 %copy-start.3 = (bf16[32,3584]{1,0:T(8,128)(2,1)S(1)}, bf16[32,3584]{1,0:T(8,128)(2,1)}, u32[]{:S(2)}) copy-start(bf16[32,3584]{1,0:T(8,128)(2,1)} %param.9) | copy-start | bytes 688132
  7.2 97.1 %reduce-scatter.4.cloned.1.call-start = ((), (), s32[]{:S(2)}) async-start(), calls=%async_computation.2 | async-start | bytes 786432 | tf_op jit(solution)/shard_map/reduce_scatter | solution.py:104
  7.2 9.4 %collective-permute-start = (bf16[32,3584]{1,0:T(8,128)(2,1)}, bf16[32,3584]{1,0:T(8,128)(2,1)S(1)}, u32[]{:S(2)}, u32[]{:S(2)}) collective-permute-start(bf16[32,3584]{1,0:T(8,128)(2,1)} %param.9), channel_id=1, source_target_pairs={{0,2},{2,4},{4,6},{6,8},{8,10},{10,12},{12,14},{14,16},{16,18},{18... | collective-permute-start | bytes 688136 | tf_op jit(solution)/shard_map/ppermute | solution.py:98
  16.7 8.1 %collective-permute-start.1 = (bf16[32,3584]{1,0:T(8,128)(2,1)S(1)}, bf16[32,3584]{1,0:T(8,128)(2,1)S(1)}, u32[]{:S(2)}, u32[]{:S(2)}) collective-permute-start(bf16[32,3584]{1,0:T(8,128)(2,1)S(1)} %collective-permute-done), channel_id=1, source_target_pairs={{0,2},{2,4},{4,6},{6,8},{8,10},{10,12},{12,14},{14,16},{16,18},{18... | collective-permute-start | bytes 688136 | tf_op jit(solution)/shard_map/ppermute | solution.py:98
  16.7 8.3 %collective-permute-start.8 = (bf16[32,3584]{1,0:T(8,128)(2,1)}, bf16[32,3584]{1,0:T(8,128)(2,1)S(1)}, u32[]{:S(2)}, u32[]{:S(2)}) collective-permute-start(bf16[32,3584]{1,0:T(8,128)(2,1)} %param.9), channel_id=1, source_target_pairs={{0,30},{2,0},{4,2},{6,4},{8,6},{10,8},{12,10},{14,12},{16,14},{18,... | collective-permute-start | bytes 688136 | tf_op jit(solution)/shard_map/ppermute | solution.py:100
  24.8 8.2 %collective-permute-start.2 = (bf16[32,3584]{1,0:T(8,128)(2,1)S(1)}, bf16[32,3584]{1,0:T(8,128)(2,1)S(1)}, u32[]{:S(2)}, u32[]{:S(2)}) collective-permute-start(bf16[32,3584]{1,0:T(8,128)(2,1)S(1)} %collective-permute-done.1), channel_id=1, source_target_pairs={{0,2},{2,4},{4,6},{6,8},{8,10},{10,12},{12,14},{14,16},{16,18},{18... | collective-permute-start | bytes 688136 | tf_op jit(solution)/shard_map/ppermute | solution.py:98
  25.0 8.1 %collective-permute-start.9 = (bf16[32,3584]{1,0:T(8,128)(2,1)S(1)}, bf16[32,3584]{1,0:T(8,128)(2,1)S(1)}, u32[]{:S(2)}, u32[]{:S(2)}) collective-permute-start(bf16[32,3584]{1,0:T(8,128)(2,1)S(1)} %collective-permute-done.8), channel_id=1, source_target_pairs={{0,30},{2,0},{4,2},{6,4},{8,6},{10,8},{12,10},{14,12},{16,14},{18,... | collective-permute-start | bytes 688136 | tf_op jit(solution)/shard_map/ppermute | solution.py:100
  33.1 8.2 %collective-permute-start.3 = (bf16[32,3584]{1,0:T(8,128)(2,1)S(1)}, bf16[32,3584]{1,0:T(8,128)(2,1)S(1)}, u32[]{:S(2)}, u32[]{:S(2)}) collective-permute-start(bf16[32,3584]{1,0:T(8,128)(2,1)S(1)} %collective-permute-done.2), channel_id=1, source_target_pairs={{0,2},{2,4},{4,6},{6,8},{8,10},{10,12},{12,14},{14,16},{16,18},{18... | collective-permute-start | bytes 688136 | tf_op jit(solution)/shard_map/ppermute | solution.py:98
  33.1 8.2 %collective-permute-start.10 = (bf16[32,3584]{1,0:T(8,128)(2,1)S(1)}, bf16[32,3584]{1,0:T(8,128)(2,1)S(1)}, u32[]{:S(2)}, u32[]{:S(2)}) collective-permute-start(bf16[32,3584]{1,0:T(8,128)(2,1)S(1)} %collective-permute-done.9), channel_id=1, source_target_pairs={{0,30},{2,0},{4,2},{6,4},{8,6},{10,8},{12,10},{14,12},{16,14},{18,... | collective-permute-start | bytes 688136 | tf_op jit(solution)/shard_map/ppermute | solution.py:100
  41.3 8.2 %collective-permute-start.4 = (bf16[32,3584]{1,0:T(8,128)(2,1)S(1)}, bf16[32,3584]{1,0:T(8,128)(2,1)S(1)}, u32[]{:S(2)}, u32[]{:S(2)}) collective-permute-start(bf16[32,3584]{1,0:T(8,128)(2,1)S(1)} %collective-permute-done.3), channel_id=1, source_target_pairs={{0,2},{2,4},{4,6},{6,8},{8,10},{10,12},{12,14},{14,16},{16,18},{18... | collective-permute-start | bytes 688136 | tf_op jit(solution)/shard_map/ppermute | solution.py:98
  41.4 9.3 %collective-permute-start.11 = (bf16[32,3584]{1,0:T(8,128)(2,1)S(1)}, bf16[32,3584]{1,0:T(8,128)(2,1)S(1)}, u32[]{:S(2)}, u32[]{:S(2)}) collective-permute-start(bf16[32,3584]{1,0:T(8,128)(2,1)S(1)} %collective-permute-done.10), channel_id=1, source_target_pairs={{0,30},{2,0},{4,2},{6,4},{8,6},{10,8},{12,10},{14,12},{16,14},{18,... | collective-permute-start | bytes 688136 | tf_op jit(solution)/shard_map/ppermute | solution.py:100
  49.6 8.3 %copy-start.4 = (bf16[32,3584]{1,0:T(8,128)(2,1)}, bf16[32,3584]{1,0:T(8,128)(2,1)S(1)}, u32[]{:S(2)}) copy-start(bf16[32,3584]{1,0:T(8,128)(2,1)S(1)} %collective-permute-done.4) | copy-start | bytes 688132
  49.6 8.3 %collective-permute-start.5 = (bf16[32,3584]{1,0:T(8,128)(2,1)S(1)}, bf16[32,3584]{1,0:T(8,128)(2,1)}, u32[]{:S(2)}, u32[]{:S(2)}) collective-permute-start(bf16[32,3584]{1,0:T(8,128)(2,1)S(1)} %collective-permute-done.4), channel_id=1, source_target_pairs={{0,2},{2,4},{4,6},{6,8},{8,10},{10,12},{12,14},{14,16},{16,18},{18... | collective-permute-start | bytes 688136 | tf_op jit(solution)/shard_map/ppermute | solution.py:98
  50.7 9.4 %collective-permute-start.12 = (bf16[32,3584]{1,0:T(8,128)(2,1)S(1)}, bf16[32,3584]{1,0:T(8,128)(2,1)}, u32[]{:S(2)}, u32[]{:S(2)}) collective-permute-start(bf16[32,3584]{1,0:T(8,128)(2,1)S(1)} %collective-permute-done.11), channel_id=1, source_target_pairs={{0,30},{2,0},{4,2},{6,4},{8,6},{10,8},{12,10},{14,12},{16,14},{18,... | collective-permute-start | bytes 688136 | tf_op jit(solution)/shard_map/ppermute | solution.py:100
  57.9 8.5 %collective-permute-start.6 = (bf16[32,3584]{1,0:T(8,128)(2,1)}, bf16[32,3584]{1,0:T(8,128)(2,1)}, u32[]{:S(2)}, u32[]{:S(2)}) collective-permute-start(bf16[32,3584]{1,0:T(8,128)(2,1)} %collective-permute-done.5), channel_id=1, source_target_pairs={{0,2},{2,4},{4,6},{6,8},{8,10},{10,12},{12,14},{14,16},{16,18},{18... | collective-permute-start | bytes 688136 | tf_op jit(solution)/shard_map/ppermute | solution.py:98
  59.2 25.4 %copy-start.5 = (bf16[32,3584]{1,0:T(8,128)(2,1)S(1)}, bf16[32,3584]{1,0:T(8,128)(2,1)}, u32[]{:S(2)}) copy-start(bf16[32,3584]{1,0:T(8,128)(2,1)} %copy-done.4) | copy-start | bytes 688132
  60.1 8.5 %collective-permute-start.13 = (bf16[32,3584]{1,0:T(8,128)(2,1)}, bf16[32,3584]{1,0:T(8,128)(2,1)}, u32[]{:S(2)}, u32[]{:S(2)}) collective-permute-start(bf16[32,3584]{1,0:T(8,128)(2,1)} %collective-permute-done.12), channel_id=1, source_target_pairs={{0,30},{2,0},{4,2},{6,4},{8,6},{10,8},{12,10},{14,12},{16,14},{18,... | collective-permute-start | bytes 688136 | tf_op jit(solution)/shard_map/ppermute | solution.py:100
  66.4 8.5 %collective-permute-start.7 = (bf16[32,3584]{1,0:T(8,128)(2,1)}, bf16[32,3584]{1,0:T(8,128)(2,1)}, u32[]{:S(2)}, u32[]{:S(2)}) collective-permute-start(bf16[32,3584]{1,0:T(8,128)(2,1)} %collective-permute-done.6), channel_id=1, source_target_pairs={{0,2},{2,4},{4,6},{6,8},{8,10},{10,12},{12,14},{14,16},{16,18},{18... | collective-permute-start | bytes 688136 | tf_op jit(solution)/shard_map/ppermute | solution.py:98
  68.6 21.2 %copy-start.10 = (f32[256,3584]{1,0:T(8,128)S(1)}, f32[256,3584]{1,0:T(8,128)}, u32[]{:S(2)}) copy-start(f32[256,3584]{1,0:T(8,128)} %param.10) | copy-start | bytes 11010052
  68.6 13.1 %collective-permute-start.14 = (bf16[32,3584]{1,0:T(8,128)(2,1)}, bf16[32,3584]{1,0:T(8,128)(2,1)S(1)}, u32[]{:S(2)}, u32[]{:S(2)}) collective-permute-start(bf16[32,3584]{1,0:T(8,128)(2,1)} %collective-permute-done.13), channel_id=1, source_target_pairs={{0,30},{2,0},{4,2},{6,4},{8,6},{10,8},{12,10},{14,12},{16,14},{18,... | collective-permute-start | bytes 688136 | tf_op jit(solution)/shard_map/ppermute | solution.py:100
  84.8 7.5 %copy-start.7 = (bf16[256,64]{0,1:T(8,128)(2,1)S(1)}, bf16[256,64]{0,1:T(8,128)(2,1)}, u32[]{:S(2)}) copy-start(bf16[256,64]{0,1:T(8,128)(2,1)} %param.15) | copy-start | bytes 98308
  86.8 18.6 %copy-start.6 = (bf16[256,2,128]{0,2,1:T(8,128)(2,1)S(1)}, bf16[256,2,128]{0,2,1:T(8,128)(2,1)}, u32[]{:S(2)}) copy-start(bf16[256,2,128]{0,2,1:T(8,128)(2,1)} %copy.108) | copy-start | bytes 393220
  86.9 3.0 %copy-start.1 = (bf16[1024,3584]{1,0:T(8,128)(2,1)}, bf16[1024,3584]{1,0:T(8,128)(2,1)S(1)}, u32[]{:S(2)}) copy-start(bf16[1024,3584]{1,0:T(8,128)(2,1)S(1)} %constant_dynamic-update-slice_fusion) | copy-start | bytes 22020100
  91.8 14.8 %copy-start.2 = (bf16[256,512]{1,0:T(8,128)(2,1)S(1)}, bf16[256,512]{1,0:T(8,128)(2,1)}, u32[]{:S(2)}) copy-start(bf16[256,512]{1,0:T(8,128)(2,1)} %param.14) | copy-start | bytes 786436
  91.8 121.7 %all-reduce.4.cloned.1.call-start = ((), (), s32[]{:S(2)}) async-start(), calls=%async_computation.4 | async-start | bytes 1310720
  106.5 54.3 %copy-start.8 = (f32[3584]{0:T(1024)S(1)}, f32[3584]{0:T(1024)}, u32[]{:S(2)}) copy-start(f32[3584]{0:T(1024)} %param.12) | copy-start | bytes 43012
  106.5 54.4 %copy-start.9 = (f32[256]{0:T(256)S(1)}, f32[256]{0:T(256)}, u32[]{:S(2)}) copy-start(f32[256]{0:T(256)} %param.11) | copy-start | bytes 3076
  109.4 114.4 %reduce-scatter.6.cloned.1.call-start = ((), (), s32[]{:S(2)}) async-start(), calls=%async_computation.3 | async-start | bytes 1572864 | tf_op jit(solution)/shard_map/reduce_scatter | solution.py:123
Sparse Core Ops, SparseCore 0:
  91.9 12.3 reduce-scatter.3
  109.5 91.8 all-reduce.3
  203.6 20.1 reduce-scatter.5
